TPU v7x, 256 devices: a whole 4x4x8 slice. The times are simulated.
256 devices in a mesh: seq: 64 (over x, z, core), head: 4 (over y).
Axes of the slice: x: 4, y: 4, z: 8, core: 2. Of those that a mesh axis runs over, the one named last changes fastest.
Arguments:
- latent: bfloat16 [64, 16, 1024], P('seq'), may hold values from -6 to 6
- stem_weight: bfloat16 [192, 3072], replicated, may hold values from -0.4375 to 0.4375
- stem_bias: float32 [3072], replicated, may hold values from -6 to 6
- mod_shift: float32 [3072], replicated, may hold values from -3 to 3
- mod_scale: float32 [3072], replicated, may hold values from -3 to 3
- qkv_weight: bfloat16 [3072, 3, 12, 128], P(None, None, 'head'), may hold values from -0.109375 to 0.109375
- q_gain: float32 [128], replicated, may hold values from 0.1 to 1.9
- k_gain: float32 [128], replicated, may hold values from 0.1 to 1.9
- tile_lists: int32 [128, 4], replicated, may hold values from 0 to 127, as said below
- out_grad: bfloat16 [16384, 12, 128], P('seq', 'head'), may hold values from -0.125 to 0.125
Outputs:
- qkv_weight_grad: float32 [3072, 3, 12, 128], P('seq', None, 'head')
- stem_weight_grad: float32 [192, 3072], P(None, 'head')
- vector_grad: float32 [3, 3072], P(None, 'head')
Inputs may be any that keep to these rules, and one draw needn't show every extreme that they name: `tile_lists`: row b holds 4 different tiles of tile b's own group of 8 tiles (b - b % 8 to b - b % 8 + 7), the first being b itself.
All inputs are finite; a program needn't handle non-finite values.
Results may differ from a plain program's by a relative error of at most 0.0078.
Values may be sent and summed in bfloat16 or wider, within the bound.
No kernel may reach another device: no remote copies, remote signals or barrier semaphores. Data moves between devices by JAX's collectives and lax.ppermute only.
A program may use at most 128 MiB of HBM per device.

v0:
```python
import jax
import jax.numpy as jnp
from jax import lax
from jax.sharding import PartitionSpec as P

TT = 2
TS = 8
KNB = 4
HG = 32
WG = 16
ln_eps = 1e-06


def swapped(value, axis, distance):
    mask = 2**distance
    pairs = [(source, source ^ mask) for source in range(lax.axis_size(axis))]
    return lax.ppermute(value, axis, pairs)


def from_behind(value, axis, steps):
    count = lax.axis_size(axis)
    first, last = (max(0, -steps), min(count, count - steps))
    return lax.ppermute(value, axis, [(source, source + steps) for source in range(first, last)])


def frames_to_tiles(blocks, row_total, col_total, tile_side):
    frames = blocks.shape[0]
    remain = blocks.shape[2:]
    shaped = blocks.reshape(
        (frames, row_total // tile_side, tile_side, col_total // tile_side, tile_side) + remain
    )
    shaped = jnp.transpose(shaped, (1, 3, 0, 2, 4) + tuple(range(5, 5 + len(remain))))
    return shaped.reshape(
        (row_total // tile_side * (col_total // tile_side), frames * tile_side * tile_side) + remain
    )


def tiles_to_frames(blocks, frames, row_total, col_total, tile_side):
    remain = blocks.shape[2:]
    shaped = blocks.reshape(
        (row_total // tile_side, col_total // tile_side, frames, tile_side, tile_side) + remain
    )
    shaped = jnp.transpose(shaped, (2, 0, 3, 1, 4) + tuple(range(5, 5 + len(remain))))
    return shaped.reshape((frames, row_total * col_total) + remain)


def qk_norm(raw_values, gain_vector):
    return (
        raw_values
        * lax.rsqrt(jnp.mean(raw_values * raw_values, -1, keepdims=True) + ln_eps)
        * gain_vector
    )


def norm_back(feature_grad, normed, inv_std, mod_scale):
    scaled = feature_grad * (1.0 + mod_scale)
    return (
        scaled
        - jnp.mean(scaled, -1, keepdims=True)
        - normed * jnp.mean(scaled * normed, -1, keepdims=True)
    ) * inv_std


def attend(queries, out_grads, key_vals, values, score_scale):
    scores = (
        jnp.einsum("brhe,bmhe->bhrm", queries, key_vals, preferred_element_type=jnp.float32)
        * score_scale
    )
    weights = jnp.exp(scores)
    probability = weights / jnp.sum(weights, axis=-1, keepdims=True)
    rounded = probability.astype(jnp.bfloat16)
    slopes = jnp.einsum("brhe,bmhe->bhrm", out_grads, values, preferred_element_type=jnp.float32)
    centre = jnp.sum(probability * slopes, axis=-1, keepdims=True)
    shaped = (probability * (slopes - centre)).astype(jnp.bfloat16)
    query_grad = (
        jnp.einsum("bhrm,bmhe->brhe", shaped, key_vals, preferred_element_type=jnp.float32)
        * score_scale
    )
    key_grad = (
        jnp.einsum("bhrm,brhe->bmhe", shaped, queries, preferred_element_type=jnp.float32)
        * score_scale
    )
    value_grad = jnp.einsum(
        "bhrm,brhe->bmhe", rounded, out_grads, preferred_element_type=jnp.float32
    )
    return (query_grad, key_grad, value_grad)


def group_share(blocks):
    seq_place = lax.axis_index("seq")
    for bit_index in range((2 * TT).bit_length() - 1):
        partner = swapped(blocks, "seq", bit_index)
        is_lower = seq_place // (1 << bit_index) % 2 == 0
        first_half = jnp.where(is_lower, blocks, partner)
        second_half = jnp.where(is_lower, partner, blocks)
        blocks = jnp.concatenate([first_half, second_half], 0)
    return blocks


def group_return(blocks):
    seq_place = lax.axis_index("seq")
    for bit_index in reversed(range((2 * TT).bit_length() - 1)):
        half_size = blocks.shape[0] // 2
        is_lower = seq_place // (1 << bit_index) % 2 == 0
        kept_part = jnp.where(is_lower, blocks[:half_size], blocks[half_size:])
        sent_part = jnp.where(is_lower, blocks[half_size:], blocks[:half_size])
        blocks = kept_part + swapped(sent_part, "seq", bit_index)
    return blocks[0]


def seq_total(stem_part, vector_part):
    return lax.psum((stem_part, vector_part), "seq")


def per_device(
    latent,
    stem_weight,
    stem_bias,
    mod_shift,
    mod_scale,
    qkv_weight,
    q_gain,
    k_gain,
    tile_lists,
    out_grad,
):
    half_rows = HG // 2
    tok_count = half_rows * WG
    frame_tokens = HG * WG
    model_width = qkv_weight.shape[0]
    heads_here = qkv_weight.shape[2]
    head_dim = qkv_weight.shape[3]
    score_scale = head_dim ** (-0.5)
    before = from_behind(latent, "seq", 2)
    after = from_behind(latent, "seq", -2)
    padded = jnp.concatenate([before, latent, after], 0)
    channels = latent.shape[1]
    patches = padded.reshape(3, channels, half_rows, 2, WG, 2)
    patches = jnp.transpose(patches, (2, 4, 0, 1, 3, 5)).reshape(tok_count, 12 * channels)
    embedded = jnp.dot(patches, stem_weight, preferred_element_type=jnp.float32) + stem_bias
    centred = embedded - jnp.mean(embedded, -1, keepdims=True)
    inv_std = lax.rsqrt(jnp.mean(centred * centred, -1, keepdims=True) + ln_eps)
    normed = centred * inv_std
    hidden = (normed * (1.0 + mod_scale) + mod_shift).astype(jnp.bfloat16)
    columns = 3 * heads_here * head_dim
    flat_weight = qkv_weight.reshape(model_width, columns)
    projected = jnp.dot(hidden, flat_weight, preferred_element_type=jnp.float32).reshape(
        tok_count, 3, heads_here, head_dim
    )
    q_normed, q_back = jax.vjp(lambda raw_values: qk_norm(raw_values, q_gain), projected[:, 0])
    k_normed, k_back = jax.vjp(lambda raw_values: qk_norm(raw_values, k_gain), projected[:, 1])
    queries = q_normed.astype(jnp.bfloat16)
    key_vals = k_normed.astype(jnp.bfloat16)
    values = projected[:, 2].astype(jnp.bfloat16)
    seq_place = lax.axis_index("seq")
    group_devs = 2 * TT
    my_group = seq_place // group_devs
    my_half = seq_place % 2
    tiles_group = HG // TS * (WG // TS)
    half_tiles = tiles_group // 2
    local_lists = (
        lax.dynamic_slice_in_dim(tile_lists, my_group * tiles_group, tiles_group, 0)
        - my_group * tiles_group
    )
    shared = group_share(jnp.stack([key_vals, values], 1)[None])
    shared = shared.reshape((TT, frame_tokens) + shared.shape[2:])
    tiles = frames_to_tiles(shared, HG, WG, TS)
    tile_len = tiles.shape[1]
    my_lists = lax.dynamic_slice_in_dim(local_lists, my_half * half_tiles, half_tiles, 0)
    near_tiles = jnp.take(tiles, my_lists.reshape(-1), axis=0)
    near_tiles = near_tiles.reshape(half_tiles, KNB * tile_len, 2, heads_here, head_dim)
    own_queries = frames_to_tiles(queries[None], half_rows, WG, TS)
    own_grads = frames_to_tiles(out_grad[None], half_rows, WG, TS)
    query_part, key_part, value_part = attend(
        own_queries, own_grads, near_tiles[:, :, 0], near_tiles[:, :, 1], score_scale
    )
    query_grad = tiles_to_frames(query_part, 1, half_rows, WG, TS)[0]
    pair_part = jnp.stack([key_part, value_part], 2).reshape(
        half_tiles * KNB, tile_len, 2, heads_here, head_dim
    )
    pair_tiles = (
        jnp.zeros((tiles_group, tile_len, 2, heads_here, head_dim), jnp.float32)
        .at[my_lists.reshape(-1)]
        .add(pair_part)
    )
    framed = tiles_to_frames(pair_tiles, TT, HG, WG, TS)
    returned = group_return(framed.reshape((group_devs, tok_count) + framed.shape[2:]))
    key_grad = returned[:, 0]
    value_grad = returned[:, 1]
    raw_q = q_back(query_grad)[0]
    raw_k = k_back(key_grad)[0]
    mixed_grad = (
        jnp.stack([raw_q, raw_k, value_grad], 1).astype(jnp.bfloat16).reshape(tok_count, columns)
    )
    weight_grad = lax.psum_scatter(
        lax.dot_general(
            hidden, mixed_grad, (((0,), (0,)), ((), ())), preferred_element_type=jnp.float32
        ),
        "seq",
        scatter_dimension=0,
        tiled=True,
    )
    weight_grad = weight_grad.reshape(-1, 3, heads_here, head_dim)
    feature_grad = lax.dot_general(
        mixed_grad, flat_weight, (((1,), (1,)), ((), ())), preferred_element_type=jnp.float32
    )
    patch_rows = patches.astype(jnp.float32)
    feature_grad = lax.psum(feature_grad, "head")
    embed_grad = norm_back(feature_grad, normed, inv_std, mod_scale)
    share_cols = model_width // lax.axis_size("head")
    offset = lax.axis_index("head") * share_cols
    grad_slice = lax.dynamic_slice_in_dim(feature_grad, offset, share_cols, 1)
    normed_slice = lax.dynamic_slice_in_dim(normed, offset, share_cols, 1)
    embed_slice = lax.dynamic_slice_in_dim(embed_grad, offset, share_cols, 1)
    stem_part = lax.dot_general(
        patch_rows, embed_slice, (((0,), (0,)), ((), ())), precision=lax.Precision.HIGHEST
    )
    vector_part = jnp.stack(
        [jnp.sum(grad_slice, 0), jnp.sum(grad_slice * normed_slice, 0), jnp.sum(embed_slice, 0)]
    )
    stem_grad, vector_grad = seq_total(stem_part, vector_part)
    return (weight_grad, stem_grad, vector_grad)


def solution(mesh):
    return jax.shard_map(
        per_device,
        mesh=mesh,
        in_specs=(
            P("seq", None, None),
            P(),
            P(),
            P(),
            P(),
            P(None, None, "head", None),
            P(),
            P(),
            P(),
            P("seq", "head", None),
        ),
        out_specs=(P("seq", None, "head", None), P(None, "head"), P(None, "head")),
        check_vma=False,
    )
```

profile of v0, /device:TPU:8, one launch (start us, length us, event | category | flops | bytes accessed | tf_op | source)
XLA Modules:
  0.0 514.7 jit_solution(13901229938263370222)
XLA Ops:
  8.1 4.0 collective-permute-start
  12.0 1.3 collective-permute-start.1
  13.3 0.7 broadcast_add_fusion
  14.0 10.3 %copy.44 = bf16[3072,3,3,128]{0,3,2,1:T(8,128)(2,1)} copy(bf16[3072,3,3,128]{3,0,2,1:T(8,128)(2,1)} %param.15) | data formatting | bytes 14155776 | tf_op args[5]
  24.7 1.7 copy.42
  26.4 0.7 reshape.189
  27.1 0.7 fusion.29
  28.3 1.1 copy-done.2
  29.4 0.5 subtract_multiply_fusion
  30.4 0.9 slice-done.3
  31.3 2.3 fusion
  34.0 0.7 copy-done.8
  35.6 1.1 collective-permute-done.2
  36.9 2.9 collective-permute-start.3
  40.2 17.6 %collective-permute-done.3 = bf16[2,256,2,3,128]{4,1,3,2,0:T(8,128)(2,1)} collective-permute-done((bf16[2,256,2,3,128]{4,1,3,2,0:T(8,128)(2,1)S(1)}, bf16[2,256,2,3,128]{4,1,3,2,0:T(8,128)(2,1)}, u32[]{:S(2)}, u32[]{:S(2)}) %collective-permute-start.3) | collective-permute-done | bytes 786464 | tf_op jit(solution)/shard_map/ppermute | solution.py:17
  57.7 1.2 broadcast_select_fusion.1
  59.7 2.6 gather_fusion
  62.3 2.3 copy.48
  64.6 0.5 copy_select_fusion
  65.1 0.7 fusion.2
  65.8 1.0 copy-done.6
  66.8 0.7 multiply_exponential_fusion
  67.5 3.3 convolution_bitcast_fusion.1
  70.8 2.1 fusion.4
  73.0 1.9 copy.54
  75.2 0.9 copy-done.11
  76.0 0.6 multiply_bitcast_fusion
  76.7 2.3 copy.53
  79.0 3.3 pad_maximum_fusion
  82.3 3.1 copy.55
  85.7 9.3 %scatter_fusion = f32[8,128,2,3,128]{4,1,3,2,0:T(8,128)S(1)} fusion(f32[8,128,2,3,128]{4,1,3,2,0:T(8,128)S(1)} %broadcast_in_dim.47, s32[16]{0:T(128)S(1)} %fusion.24, f32[16,128,2,3,128]{4,1,3,2,0:T(8,128)} %copy.55), kind=kCustom, calls=%fused_computation.1 | custom fusion | flops 1572864 | bytes 18874432 | tf_op jit(solution)/shard_map/scatter-add | solution.py:184
  95.9 1.8 collective-permute-start.4
  97.7 34.2 %collective-permute-done.4 = f32[2,256,2,3,128]{4,1,3,2,0:T(8,128)S(1)} collective-permute-done((f32[2,256,2,3,128]{4,1,3,2,0:T(8,128)S(1)}, f32[2,256,2,3,128]{4,1,3,2,0:T(8,128)S(1)}, u32[]{:S(2)}, u32[]{:S(2)}) %collective-permute-start.4) | collective-permute-done | bytes 1572896 | tf_op jit(solution)/shard_map/ppermute | solution.py:17
  132.3 1.8 copy-done.7
  135.6 0.6 copy-done.13
  136.3 4.0 convolution_bitcast_fusion
  140.6 2.1 maximum_convert_fusion
  142.7 2.1 copy.59
  144.8 8.4 %fusion.14 = f32[3072,1152]{1,0:T(8,128)} fusion(bf16[256,1152]{0,1:T(8,128)(2,1)} %bitcast.148, f32[256,3072]{1,0:T(8,128)S(1)} %copy-done.5, f32[3072]{0:T(1024)S(1)} %copy-done.17, f32[3072]{0:T(1024)S(1)} %broadcast_add_fusion), kind=kOutput, calls=%fused_computation.48 | convolution fusion | flops 1814298624 | bytes 17915904 | tf_op jit(solution)/shard_map/dot_general | solution.py:196
  153.3 70.6 %all-reduce.3.cloned.1.call-done = f32[256,3072]{1,0:T(8,128)} async-done(((f32[256,3072]{1,0:T(8,128)}), f32[256,3072]{1,0:T(8,128)}) %all-reduce.3.cloned.1.call-update) | async-done | bytes 3145744 | tf_op jit(solution)/shard_map/psum | solution.py:208
  223.9 2.9 fusion.26
  226.8 1.7 dynamic-slice_reduce_fusion
  228.5 1.3 fusion.30
  229.9 252.3 %psum.23 = f32[3,768]{1,0:T(4,128)} all-reduce(f32[3,768]{1,0:T(4,128)S(1)} %pad_maximum_fusion.4), channel_id=1, replica_groups=mesh['seq'=64,'head'=4] {'seq'}, use_global_device_ids=true, to_apply=%region_17.18 | all-reduce | flops 2304 | bytes 18432 | tf_op jit(solution)/shard_map/psum | solution.py:112
  482.2 1.0 reshape.197
  483.3 0.7 copy.60
  484.0 21.3 %all-reduce.5.cloned.1.call-done = f32[192,768]{1,0:T(8,128)} async-done(((f32[192,768]{1,0:T(8,128)}), f32[192,768]{1,0:T(8,128)}) %all-reduce.5.cloned.1.call-update) | async-done | bytes 589840 | tf_op jit(solution)/shard_map/psum | solution.py:112
  505.3 1.9 copy.73
  (109 shorter events, 7.6 us)
Async XLA Ops:
  8.0 19.1 %copy-start = (bf16[192,3072]{1,0:T(8,128)(2,1)S(1)}, bf16[192,3072]{1,0:T(8,128)(2,1)}, u32[]{:S(2)}) copy-start(bf16[192,3072]{1,0:T(8,128)(2,1)} %param.11) | copy-start | bytes 3538948
  8.0 215.9 %all-reduce.3.cloned.1.call-start = ((), (), s32[]{:S(2)}) async-start(), calls=%async_computation.2 | async-start | bytes 6291456 | tf_op jit(solution)/shard_map/psum | solution.py:208
  8.1 16.3 %collective-permute-start = (bf16[1,16,1024]{2,1,0:T(8,128)(2,1)}, bf16[1,16,1024]{2,1,0:T(8,128)(2,1)S(1)}, u32[]{:S(2)}, u32[]{:S(2)}) collective-permute-start(bf16[1,16,1024]{2,1,0:T(8,128)(2,1)} %param.10), channel_id=1, source_target_pairs={{0,8},{4,12},{8,16},{12,20},{16,24},{20,28},{24,32},{28,36},{32,40... | collective-permute-start | bytes 98312 | tf_op jit(solution)/shard_map/ppermute | solution.py:23
  12.0 12.3 %collective-permute-start.1 = (bf16[1,16,1024]{2,1,0:T(8,128)(2,1)}, bf16[1,16,1024]{2,1,0:T(8,128)(2,1)S(1)}, u32[]{:S(2)}, u32[]{:S(2)}) collective-permute-start(bf16[1,16,1024]{2,1,0:T(8,128)(2,1)} %param.10), channel_id=1, source_target_pairs={{8,0},{12,4},{16,8},{20,12},{24,16},{28,20},{32,24},{36,28},{40,32... | collective-permute-start | bytes 98312 | tf_op jit(solution)/shard_map/ppermute | solution.py:23
  14.0 10.3 %copy-start.18 = (bf16[1,16,1024]{2,1,0:T(8,128)(2,1)S(1)}, bf16[1,16,1024]{2,1,0:T(8,128)(2,1)}, u32[]{:S(2)}) copy-start(bf16[1,16,1024]{2,1,0:T(8,128)(2,1)} %param.10) | copy-start | bytes 98308
  24.3 2.8 copy-start.19
  27.1 3.3 slice-start.2
  27.8 1.6 copy-start.2
  27.8 3.5 slice-start.3
  29.4 1.9 copy-start.17
  31.3 2.3 copy-start.4
  31.3 3.4 copy-start.20
  33.6 1.1 copy-start.8
  33.6 1.4 copy-start.22
  33.6 1.9 copy-start.16
  33.9 6.0 %copy-start.21 = (f32[128]{0:T(128)S(1)}, f32[128]{0:T(128)}, u32[]{:S(2)}) copy-start(f32[128]{0:T(128)} %param.16) | copy-start | bytes 1540
  34.9 1.8 collective-permute-start.2
  35.6 29.5 %copy-start.15 = (bf16[2,2,1,8,8,3,128]{6,4,3,5,1,0,2:T(8,128)(2,1)}, bf16[2,2,1,8,8,3,128]{6,4,3,5,1,0,2:T(8,128)(2,1)S(1)}, u32[]{:S(2)}) copy-start(bf16[2,2,1,8,8,3,128]{6,4,3,5,1,0,2:T(8,128)(2,1)S(1)} %copy.51) | copy-start | bytes 589828
  36.9 20.9 %collective-permute-start.3 = (bf16[2,256,2,3,128]{4,1,3,2,0:T(8,128)(2,1)S(1)}, bf16[2,256,2,3,128]{4,1,3,2,0:T(8,128)(2,1)}, u32[]{:S(2)}, u32[]{:S(2)}) collective-permute-start(bf16[2,256,2,3,128]{4,1,3,2,0:T(8,128)(2,1)S(1)} %pad_maximum_fusion.2), channel_id=1, source_target_pairs={{0,8},{4,12},{8,0},{12,4},{16,24},{20,28},{24,16},{28,20},{32,40},... | collective-permute-start | bytes 2359304 | tf_op jit(solution)/shard_map/ppermute | solution.py:17
  65.1 1.7 copy-start.6
  70.8 2.1 copy-start.10
  75.2 0.9 copy-start.11
  95.7 36.6 %copy-start.12 = (bf16[4,3,64,512]{3,2,1,0:T(8,128)(2,1)S(1)}, bf16[4,3,64,512]{3,2,1,0:T(8,128)(2,1)}, u32[]{:S(2)}) copy-start(bf16[4,3,64,512]{3,2,1,0:T(8,128)(2,1)} %copy-done.11) | copy-start | bytes 2359300
  95.9 36.0 %collective-permute-start.4 = (f32[2,256,2,3,128]{4,1,3,2,0:T(8,128)S(1)}, f32[2,256,2,3,128]{4,1,3,2,0:T(8,128)S(1)}, u32[]{:S(2)}, u32[]{:S(2)}) collective-permute-start(f32[2,256,2,3,128]{4,1,3,2,0:T(8,128)S(1)} %copy.57), channel_id=1, source_target_pairs={{0,8},{4,12},{8,0},{12,4},{16,24},{20,28},{24,16},{28,20},{32,40},... | collective-permute-start | bytes 4718600 | tf_op jit(solution)/shard_map/ppermute | solution.py:17
  131.9 2.2 copy-start.7
  131.9 4.5 slice-start
  132.2 2.6 copy-start.9
  132.2 4.1 slice-start.1
  132.2 2.4 collective-permute-start.5
  135.6 0.7 copy-start.13
  135.6 0.7 copy-start.14
  140.3 4.5 copy-start.5
  140.3 341.9 %reduce-scatter.2.cloned.1.call-start = ((), (), s32[]{:S(2)}) async-start(), calls=%async_computation.1 | async-start | bytes 14376960 | tf_op jit(solution)/shard_map/reduce_scatter | solution.py:195
  153.2 70.7 %copy-start.3 = (f32[256,3072]{1,0:T(8,128)S(1)}, f32[256,3072]{1,0:T(8,128)}, u32[]{:S(2)}) copy-start(f32[256,3072]{1,0:T(8,128)} %copy-done.2) | copy-start | bytes 9437188
  153.2 352.1 %all-reduce.5.cloned.1.call-start = ((), (), s32[]{:S(2)}) async-start(), calls=%async_computation.3 | async-start | bytes 1179648 | tf_op jit(solution)/shard_map/psum | solution.py:112
  226.8 280.5 %copy-start.1 = (bf16[192,3072]{1,0:T(8,128)(2,1)S(1)}, bf16[192,3072]{1,0:T(8,128)(2,1)}, u32[]{:S(2)}) copy-start(bf16[192,3072]{1,0:T(8,128)(2,1)} %param.11) | copy-start | bytes 3538948
Sparse Core Ops, SparseCore 0:
  140.5 83.3 all-reduce.2
Sparse Core Ops, SparseCore 1:
  153.3 168.1 reduce-scatter.1
  325.3 179.9 all-reduce.4
where the time goes:
time: 516 us; the launch traced here: 515 us
  blocking collectives  252 us (49%)
  waiting for transfers between devices  145 us (28%)
  local copies, waits for them, and re-layouts  40.5 us (8%)
  other arithmetic  28 us (5%)
  matrix products  22.3 us (4%)
  between operations  16.1 us (3%)
  starting transfers between devices  10.5 us (2%)
    psum x1, blocking collectives, seq_total(): return lax.psum((stem_part, vector_part), 'seq')  252 us
    psum x1, waiting for transfers between devices, per_device(): feature_grad = lax.psum(feature_grad, 'head')  70.6 us
    ppermute x4, waiting for transfers between devices, swapped(): return lax.ppermute(value, axis, pairs)  52.9 us
    psum x1, waiting for transfers between devices, seq_total(): return lax.psum((stem_part, vector_part), 'seq')  21.3 us
    unnamed x59, local copies, waits for them, and re-layouts  20.7 us
  transfers between devices with their start and end apart: 9, of which 5 were waited for; matrix products, arithmetic and copies ran while one was open for 6% of the time, Pallas kernels for 0%

commit v1 on v0

--- a/solution.py
+++ b/solution.py
@@ -205,7 +205,11 @@
         mixed_grad, flat_weight, (((1,), (1,)), ((), ())), preferred_element_type=jnp.float32
     )
     patch_rows = patches.astype(jnp.float32)
-    feature_grad = lax.psum(feature_grad, "head")
+    feature_grad = feature_grad
+    for hop in (1, 2):
+        feature_grad = feature_grad + lax.ppermute(
+            feature_grad, "head", [(dev, dev ^ hop) for dev in range(4)]
+        )
     embed_grad = norm_back(feature_grad, normed, inv_std, mod_scale)
     share_cols = model_width // lax.axis_size("head")
     offset = lax.axis_index("head") * share_cols

time: 516 us -> 567 us (1.099)
  waiting for transfers between devices: 145 us -> 192 us
    ppermute x0 -> x2, waiting for transfers between devices: none -> 139 us  [per_device(): lax.ppermute(feature_grad, 'head', [(dev, dev ^ hop) for dev in range(4)])]
    psum x1 -> x0, waiting for transfers between devices: 70.6 us -> none  [per_device(): feature_grad = lax.psum(feature_grad, 'head')]
    psum x1, waiting for transfers between devices: 21.3 us -> 0.01 us  [seq_total(): return lax.psum((stem_part, vector_part), 'seq')]
  transfers between devices with their start and end apart: 9 -> 10, of which waited for: 5 -> 6; matrix products, arithmetic and copies ran while one was open for 6% -> 5% of each run, Pallas kernels for 0% -> 0%
where the time goes in v1:
time: 567 us; the launch traced here: 566 us
  blocking collectives  252 us (44%)
  waiting for transfers between devices  192 us (34%)
  local copies, waits for them, and re-layouts  41.1 us (7%)
  other arithmetic  29.9 us (5%)
  matrix products  23.6 us (4%)
  between operations  14.7 us (3%)
  starting transfers between devices  13.3 us (2%)
    psum x1, blocking collectives, seq_total(): return lax.psum((stem_part, vector_part), 'seq')  252 us
    ppermute x2, waiting for transfers between devices, per_device(): lax.ppermute(feature_grad, 'head', [(dev, dev ^ hop) for dev in range(4)])  139 us
    ppermute x4, waiting for transfers between devices, swapped(): return lax.ppermute(value, axis, pairs)  53.2 us
    unnamed x59, local copies, waits for them, and re-layouts  21.2 us
  transfers between devices with their start and end apart: 10, of which 6 were waited for; matrix products, arithmetic and copies ran while one was open for 5% of the time, Pallas kernels for 0%

profile of v1, /device:TPU:8, one launch (start us, length us, event | category | flops | bytes accessed | tf_op | source)
XLA Modules:
  0.0 566.2 jit_solution(9737625891737487773)
XLA Ops:
  7.2 4.0 collective-permute-start
  11.2 1.3 collective-permute-start.1
  12.5 0.7 broadcast_add_fusion
  13.2 10.3 %copy.44 = bf16[3072,3,3,128]{0,3,2,1:T(8,128)(2,1)} copy(bf16[3072,3,3,128]{3,0,2,1:T(8,128)(2,1)} %param.15) | data formatting | bytes 14155776 | tf_op args[5]
  23.9 1.7 copy.42
  25.6 0.7 reshape.189
  26.3 0.7 fusion.29
  27.5 1.1 copy-done.2
  29.6 0.9 slice-done.1
  30.5 2.3 fusion
  33.1 0.7 copy-done.8
  34.8 1.1 collective-permute-done.2
  36.0 2.9 collective-permute-start.3
  39.3 17.6 %collective-permute-done.3 = bf16[2,256,2,3,128]{4,1,3,2,0:T(8,128)(2,1)} collective-permute-done((bf16[2,256,2,3,128]{4,1,3,2,0:T(8,128)(2,1)S(1)}, bf16[2,256,2,3,128]{4,1,3,2,0:T(8,128)(2,1)}, u32[]{:S(2)}, u32[]{:S(2)}) %collective-permute-start.3) | collective-permute-done | bytes 786464 | tf_op jit(solution)/shard_map/ppermute | solution.py:17
  56.9 1.2 broadcast_select_fusion.1
  58.9 2.6 gather_fusion
  61.5 2.3 copy.48
  64.3 0.7 fusion.2
  65.0 1.0 copy-done.6
  66.0 0.7 multiply_exponential_fusion
  66.7 3.3 convolution_bitcast_fusion.1
  70.0 2.1 fusion.4
  72.1 1.9 copy.54
  74.3 0.9 copy-done.11
  75.8 2.3 copy.53
  78.2 3.3 pad_maximum_fusion
  81.4 3.1 copy.55
  84.9 9.3 %scatter_fusion = f32[8,128,2,3,128]{4,1,3,2,0:T(8,128)S(1)} fusion(f32[8,128,2,3,128]{4,1,3,2,0:T(8,128)S(1)} %broadcast_in_dim.47, s32[16]{0:T(128)S(1)} %fusion.24, f32[16,128,2,3,128]{4,1,3,2,0:T(8,128)} %copy.55), kind=kCustom, calls=%fused_computation.1 | custom fusion | flops 1572864 | bytes 18874432 | tf_op jit(solution)/shard_map/scatter-add | solution.py:184
  95.0 1.8 collective-permute-start.4
  96.9 34.2 %collective-permute-done.4 = f32[2,256,2,3,128]{4,1,3,2,0:T(8,128)S(1)} collective-permute-done((f32[2,256,2,3,128]{4,1,3,2,0:T(8,128)S(1)}, f32[2,256,2,3,128]{4,1,3,2,0:T(8,128)S(1)}, u32[]{:S(2)}, u32[]{:S(2)}) %collective-permute-start.4) | collective-permute-done | bytes 1572896 | tf_op jit(solution)/shard_map/ppermute | solution.py:17
  131.7 1.2 copy-done.7
  135.0 0.7 copy-done.13
  135.7 0.9 maximum_convert_fusion
  136.6 2.1 copy.59
  138.7 8.4 %fusion.14 = f32[3072,1152]{1,0:T(8,128)} fusion(bf16[256,1152]{0,1:T(8,128)(2,1)} %bitcast.146, f32[256,3072]{1,0:T(8,128)S(1)} %copy-done.5, f32[3072]{0:T(1024)S(1)} %copy-done.19, f32[3072]{0:T(1024)S(1)} %broadcast_add_fusion), kind=kOutput, calls=%fused_computation.48 | convolution fusion | flops 1814298624 | bytes 17915904 | tf_op jit(solution)/shard_map/dot_general | solution.py:196
  147.2 0.8 copy-done.14
  148.1 5.3 convolution_bitcast_fusion
  153.9 69.7 %collective-permute-done.6 = f32[256,3072]{1,0:T(8,128)S(1)} collective-permute-done((f32[256,3072]{1,0:T(8,128)S(1)}, f32[256,3072]{1,0:T(8,128)S(1)}, u32[]{:S(2)}, u32[]{:S(2)}) %collective-permute-start.6) | collective-permute-done | bytes 3145760 | tf_op jit(solution)/shard_map/ppermute | solution.py:210
  223.6 2.2 add.131
  225.8 2.3 collective-permute-start.7
  228.2 68.8 %collective-permute-done.7 = f32[256,3072]{1,0:T(8,128)} collective-permute-done((f32[256,3072]{1,0:T(8,128)}, f32[256,3072]{1,0:T(8,128)}, u32[]{:S(2)}, u32[]{:S(2)}) %collective-permute-start.7) | collective-permute-done | bytes 3145760 | tf_op jit(solution)/shard_map/ppermute | solution.py:210
  297.0 3.9 fusion.26
  300.9 1.5 dynamic-slice_reduce_fusion
  302.5 1.3 fusion.30
  303.8 251.8 %psum.15 = f32[3,768]{1,0:T(4,128)} all-reduce(f32[3,768]{1,0:T(4,128)S(1)} %pad_maximum_fusion.4), channel_id=1, replica_groups=mesh['seq'=64,'head'=4] {'seq'}, use_global_device_ids=true, to_apply=%region_16.17 | all-reduce | flops 2304 | bytes 18432 | tf_op jit(solution)/shard_map/psum | solution.py:112
  555.7 1.0 reshape.197
  556.7 0.7 copy.60
  557.4 1.9 copy.72
  (110 shorter events, 10.4 us)
Async XLA Ops:
  7.2 19.1 %copy-start = (bf16[192,3072]{1,0:T(8,128)(2,1)S(1)}, bf16[192,3072]{1,0:T(8,128)(2,1)}, u32[]{:S(2)}) copy-start(bf16[192,3072]{1,0:T(8,128)(2,1)} %param.11) | copy-start | bytes 3538948
  7.2 548.5 %reduce-scatter.2.cloned.1.call-start = ((), (), s32[]{:S(2)}) async-start(), calls=%async_computation.1 | async-start | bytes 14376960 | tf_op jit(solution)/shard_map/reduce_scatter | solution.py:195
  7.2 16.3 %collective-permute-start = (bf16[1,16,1024]{2,1,0:T(8,128)(2,1)}, bf16[1,16,1024]{2,1,0:T(8,128)(2,1)S(1)}, u32[]{:S(2)}, u32[]{:S(2)}) collective-permute-start(bf16[1,16,1024]{2,1,0:T(8,128)(2,1)} %param.10), channel_id=1, source_target_pairs={{0,8},{4,12},{8,16},{12,20},{16,24},{20,28},{24,32},{28,36},{32,40... | collective-permute-start | bytes 98312 | tf_op jit(solution)/shard_map/ppermute | solution.py:23
  11.2 12.3 %collective-permute-start.1 = (bf16[1,16,1024]{2,1,0:T(8,128)(2,1)}, bf16[1,16,1024]{2,1,0:T(8,128)(2,1)S(1)}, u32[]{:S(2)}, u32[]{:S(2)}) collective-permute-start(bf16[1,16,1024]{2,1,0:T(8,128)(2,1)} %param.10), channel_id=1, source_target_pairs={{8,0},{12,4},{16,8},{20,12},{24,16},{28,20},{32,24},{36,28},{40,32... | collective-permute-start | bytes 98312 | tf_op jit(solution)/shard_map/ppermute | solution.py:23
  13.2 10.3 %copy-start.20 = (bf16[1,16,1024]{2,1,0:T(8,128)(2,1)S(1)}, bf16[1,16,1024]{2,1,0:T(8,128)(2,1)}, u32[]{:S(2)}) copy-start(bf16[1,16,1024]{2,1,0:T(8,128)(2,1)} %param.10) | copy-start | bytes 98308
  23.5 2.8 copy-start.21
  26.3 3.3 slice-start
  27.0 1.6 copy-start.2
  27.0 3.5 slice-start.1
  28.6 1.9 copy-start.19
  30.5 2.3 copy-start.4
  30.5 3.4 copy-start.22
  32.8 1.1 copy-start.8
  32.8 1.4 copy-start.24
  32.8 1.9 copy-start.18
  33.1 6.0 %copy-start.23 = (f32[128]{0:T(128)S(1)}, f32[128]{0:T(128)}, u32[]{:S(2)}) copy-start(f32[128]{0:T(128)} %param.16) | copy-start | bytes 1540
  34.1 1.8 collective-permute-start.2
  34.8 29.5 %copy-start.17 = (bf16[2,2,1,8,8,3,128]{6,4,3,5,1,0,2:T(8,128)(2,1)}, bf16[2,2,1,8,8,3,128]{6,4,3,5,1,0,2:T(8,128)(2,1)S(1)}, u32[]{:S(2)}) copy-start(bf16[2,2,1,8,8,3,128]{6,4,3,5,1,0,2:T(8,128)(2,1)S(1)} %copy.51) | copy-start | bytes 589828
  36.0 20.9 %collective-permute-start.3 = (bf16[2,256,2,3,128]{4,1,3,2,0:T(8,128)(2,1)S(1)}, bf16[2,256,2,3,128]{4,1,3,2,0:T(8,128)(2,1)}, u32[]{:S(2)}, u32[]{:S(2)}) collective-permute-start(bf16[2,256,2,3,128]{4,1,3,2,0:T(8,128)(2,1)S(1)} %pad_maximum_fusion.2), channel_id=1, source_target_pairs={{0,8},{4,12},{8,0},{12,4},{16,24},{20,28},{24,16},{28,20},{32,40},... | collective-permute-start | bytes 2359304 | tf_op jit(solution)/shard_map/ppermute | solution.py:17
  64.3 1.7 copy-start.6
  70.0 2.1 copy-start.10
  74.3 0.9 copy-start.11
  95.0 36.0 %collective-permute-start.4 = (f32[2,256,2,3,128]{4,1,3,2,0:T(8,128)S(1)}, f32[2,256,2,3,128]{4,1,3,2,0:T(8,128)S(1)}, u32[]{:S(2)}, u32[]{:S(2)}) collective-permute-start(f32[2,256,2,3,128]{4,1,3,2,0:T(8,128)S(1)} %copy.57), channel_id=1, source_target_pairs={{0,8},{4,12},{8,0},{12,4},{16,24},{20,28},{24,16},{28,20},{32,40},... | collective-permute-start | bytes 4718600 | tf_op jit(solution)/shard_map/ppermute | solution.py:17
  131.0 1.9 copy-start.7
  131.0 2.1 copy-start.12
  131.4 2.8 copy-start.9
  131.4 2.6 collective-permute-start.5
  134.2 4.5 copy-start.5
  135.0 0.7 copy-start.13
  135.0 0.7 copy-start.15
  147.1 0.9 copy-start.14
  147.1 1.0 copy-start.16
  147.1 410.2 %all-reduce.2.cloned.1.call-start = ((), (), s32[]{:S(2)}) async-start(), calls=%async_computation.2 | async-start | bytes 1179648 | tf_op jit(solution)/shard_map/psum | solution.py:112
  153.4 143.6 %copy-start.3 = (f32[256,3072]{1,0:T(8,128)S(1)}, f32[256,3072]{1,0:T(8,128)}, u32[]{:S(2)}) copy-start(f32[256,3072]{1,0:T(8,128)} %copy-done.2) | copy-start | bytes 9437188
  153.4 70.2 %collective-permute-start.6 = (f32[256,3072]{1,0:T(8,128)S(1)}, f32[256,3072]{1,0:T(8,128)S(1)}, u32[]{:S(2)}, u32[]{:S(2)}) collective-permute-start(f32[256,3072]{1,0:T(8,128)S(1)} %convolution_bitcast_fusion), channel_id=1, source_target_pairs={{0,1},{1,0},{2,3},{3,2},{4,5},{5,4},{6,7},{7,6},{8,9},{9,8},{10,11... | collective-permute-start | bytes 9437192 | tf_op jit(solution)/shard_map/ppermute | solution.py:210
  225.8 71.1 %collective-permute-start.7 = (f32[256,3072]{1,0:T(8,128)}, f32[256,3072]{1,0:T(8,128)}, u32[]{:S(2)}, u32[]{:S(2)}) collective-permute-start(f32[256,3072]{1,0:T(8,128)} %add.131), channel_id=1, source_target_pairs={{0,2},{1,3},{2,0},{3,1},{4,6},{5,7},{6,4},{7,5},{8,10},{9,11},{10,... | collective-permute-start | bytes 9437192 | tf_op jit(solution)/shard_map/ppermute | solution.py:210
  300.9 258.4 %copy-start.1 = (bf16[192,3072]{1,0:T(8,128)(2,1)S(1)}, bf16[192,3072]{1,0:T(8,128)(2,1)}, u32[]{:S(2)}) copy-start(bf16[192,3072]{1,0:T(8,128)(2,1)} %param.11) | copy-start | bytes 3538948
Sparse Core Ops, SparseCore 0:
  147.3 168.0 reduce-scatter.1
  319.4 180.8 all-reduce.1
